TPU v7x, 128 devices: a whole 4x4x4 slice. The times are simulated.
128 devices in a mesh: row: 8 (over y, core), col: 16 (over z, x).
Axes of the slice: x: 4, y: 4, z: 4, core: 2. Of those that a mesh axis runs over, the one named last changes fastest.
Arguments:
- b_three: bfloat16 [256, 384, 1536], P(('row', 'col')), may hold values from -0.47851562 to 0.47851562
- e_occ: float32 [256], replicated, may hold values from -1.5 to -0.3
- e_vir: float32 [384], replicated, may hold values from 0.2 to 3
- c_occ: bfloat16 [768, 256], replicated, may hold values from -0.375 to 0.375
- pair_list: int32 [128, 16, 2], P(('row', 'col')), may hold values from 0 to 255, as said below
- pair_live: int32 [128, 16], P(('row', 'col')), may hold values from 0 to 1, as said below
Outputs:
- gamma_ao: bfloat16 [384, 1536, 768], P('row', 'col')
Inputs may be any that keep to these rules, and one draw needn't show every extreme that they name: pair_list[w, p, 0] is one of the orbitals 2 w to 2 w + 1; pair_list[w, p, 1] is one of the orbitals 2 q to 2 q + 1 with q = (w // 16) * 16 + p. `pair_live`: every worker lists between 1 and 16 pairs; some worker lists all 16.
All inputs are finite; a program needn't handle non-finite values.
Results may differ from a plain program's by a relative error of at most 0.0053.
Values may be sent and summed in bfloat16 or wider, within the bound.
No kernel may reach another device: no remote copies, remote signals or barrier semaphores. Data moves between devices by JAX's collectives and lax.ppermute only.
A program may use at most 128 MiB of HBM per device.

v0:
```python
import jax
import jax.numpy as jnp
from jax import lax
from jax.sharding import PartitionSpec as P


def local(b_three, e_occ, e_vir, c_occ, pair_list, pair_live):
    own_count = b_three.shape[0]
    virt_count = b_three.shape[1]
    aux_count = b_three.shape[2]
    peer_count = lax.axis_size("col")
    row_count = lax.axis_size("row")

    def pair_step(gamma, peer, right_slab):
        first_orb = pair_list[0, peer, 0]
        second_orb = pair_list[0, peer, 1]
        listed_flag = pair_live[0, peer]
        own_slot = first_orb % own_count
        left_slab = lax.dynamic_index_in_dim(b_three, own_slot, 0, keepdims=False)
        integrals = lax.dot_general(
            left_slab, right_slab, (((1,), (1,)), ((), ())), preferred_element_type=jnp.float32
        )
        denominator = e_occ[first_orb] + e_occ[second_orb] - e_vir[:, None] - e_vir[None, :]
        amplitude = integrals / denominator
        weighted = (2.0 * amplitude - amplitude.T).astype(jnp.bfloat16)
        addition = jnp.dot(weighted, right_slab, preferred_element_type=jnp.float32)
        current = lax.dynamic_index_in_dim(gamma, own_slot, 0, keepdims=False)
        return lax.dynamic_update_index_in_dim(
            gamma, current + listed_flag.astype(jnp.float32) * addition, own_slot, 0
        )

    gamma = jnp.zeros(b_three.shape, jnp.float32)

    def fold_peers(gamma, piece):
        count = piece.shape[0] // own_count

        def visit(position, gamma):
            wanted = pair_list[0, position, 1] % own_count
            right_slab = lax.dynamic_index_in_dim(
                piece, position * own_count + wanted, 0, keepdims=False
            )
            return pair_step(gamma, position, right_slab)

        return lax.fori_loop(0, count, visit, gamma)

    gamma = fold_peers(gamma, lax.all_gather(b_three, "col", axis=0, tiled=True))
    gamma_mo = gamma.astype(jnp.bfloat16)
    virt_local = virt_count // row_count
    aux_local = aux_count // peer_count
    total_orbs = c_occ.shape[1]
    blocks = gamma_mo.reshape(own_count, row_count, virt_local, peer_count, aux_local)
    blocks = jnp.transpose(blocks, (1, 3, 0, 2, 4)).reshape(
        row_count * peer_count, own_count, virt_local * aux_local
    )
    regrouped = lax.all_to_all(blocks, ("row", "col"), split_axis=0, concat_axis=0, tiled=True)
    moved = regrouped.reshape(total_orbs, virt_local * aux_local)
    result = lax.dot_general(
        moved, c_occ, (((0,), (1,)), ((), ())), preferred_element_type=jnp.float32
    ).astype(jnp.bfloat16)
    return result.reshape(virt_local, aux_local, c_occ.shape[0])


def solution(mesh):
    return jax.shard_map(
        local,
        mesh=mesh,
        in_specs=(
            P(("row", "col"), None, None),
            P(),
            P(),
            P(),
            P(("row", "col"), None, None),
            P(("row", "col"), None),
        ),
        out_specs=P("row", "col", None),
        check_vma=False,
    )
```

profile of v0, /device:TPU:1, one launch (start us, length us, event | category | flops | bytes accessed | tf_op | source)
XLA Modules:
  0.0 638.8 jit_solution(17668714508559472050)
XLA Ops:
  7.3 223.8 %all-gather.2.cloned.1.call-done = bf16[32,384,1536]{2,1,0:T(8,128)(2,1)} async-done(((bf16[2,384,1536]{2,1,0:T(8,128)(2,1)}), bf16[32,384,1536]{2,1,0:T(8,128)(2,1)}) %all-gather.2.cloned.1.call-update) | async-done | bytes 37748752 | tf_op jit(solution)/shard_map/all_gather | solution.py:46
  231.1 2.8 broadcast_in_dim.20
  233.9 331.1 %while.15 = (s32[]{:T(128)}, f32[2,384,1536]{2,1,0:T(8,128)}, s32[1,16,2]{1,2,0:T(2,128)S(1)}, s32[1,16]{1,0:T(1,128)S(1)}, bf16[2,384,1536]{2,1,0:T(8,128)(2,1)...) while((s32[]{:T(128)}, f32[2,384,1536]{2,1,0:T(8,128)}, ...), condition=%wide.region_1.2_spmd, body=%wide.region_0.1_spmd.sunk | while | flops 908181888 | bytes 53686384 | solution.py:44
  243.8 2.4 fusion.38
  249.5 2.9 fusion.40
  270.2 2.9 fusion.40
  285.2 2.4 fusion.38
  290.9 2.9 fusion.40
  311.6 2.9 fusion.40
  326.5 2.4 fusion.38
  332.2 2.9 fusion.40
  352.9 2.9 fusion.40
  367.9 2.4 fusion.38
  373.6 2.9 fusion.40
  394.3 2.9 fusion.40
  409.3 2.4 fusion.38
  415.0 2.9 fusion.40
  435.7 2.9 fusion.40
  456.4 2.9 fusion.40
  477.1 2.9 fusion.40
  497.8 2.9 fusion.40
  518.5 2.9 fusion.40
  539.2 2.9 fusion.40
  559.8 2.9 fusion.40
  564.9 4.0 convert_element_type.29
  569.0 4.9 reshape.22
  573.9 2.5 copy.17
  576.4 5.1 reshape.23
  581.5 2.4 copy.15
  583.9 40.1 %all_to_all.5 = bf16[128,2,4608]{2,1,0:T(2,128)(2,1)} all-to-all(bf16[128,2,4608]{2,1,0:T(2,128)(2,1)S(1)} %copy.15), channel_id=1, replica_groups=mesh['row'=8,'col'=16] {'row','col'}, dimensions={0} | all-to-all | bytes 4718592 | tf_op jit(solution)/shard_map/all_to_all | solution.py:55
  624.0 2.9 reshape.24
  626.9 5.0 convolution_convert_fusion
  (183 shorter events, 146.3 us)
Async XLA Ops:
  6.5 620.4 %copy-start = (bf16[768,256]{1,0:T(8,128)(2,1)S(1)}, bf16[768,256]{1,0:T(8,128)(2,1)}, u32[]{:S(2)}) copy-start(bf16[768,256]{1,0:T(8,128)(2,1)} %param.11) | copy-start | bytes 1179652
  6.5 224.6 %all-gather.2.cloned.1.call-start = ((), (), s32[]{:S(2)}) async-start(), calls=%async_computation.1 | async-start | bytes 40108032 | tf_op jit(solution)/shard_map/all_gather | solution.py:46
  7.3 226.6 %copy-start.3 = (f32[384]{0:T(512)S(1)}, f32[384]{0:T(512)}, u32[]{:S(2)}) copy-start(f32[384]{0:T(512)} %param.10) | copy-start | bytes 4612
  7.3 226.6 %copy-start.4 = (f32[256]{0:T(256)S(1)}, f32[256]{0:T(256)}, u32[]{:S(2)}) copy-start(f32[256]{0:T(256)} %param.9) | copy-start | bytes 3076
  7.3 226.6 %copy-start.5 = (s32[1,16,2]{1,2,0:T(2,128)S(1)}, s32[1,16,2]{1,2,0:T(2,128)}, u32[]{:S(2)}) copy-start(s32[1,16,2]{1,2,0:T(2,128)} %param.12) | copy-start | bytes 388
  7.3 226.6 %copy-start.6 = (s32[1,16]{1,0:T(1,128)S(1)}, s32[1,16]{1,0:T(1,128)}, u32[]{:S(2)}) copy-start(s32[1,16]{1,0:T(1,128)} %param.13) | copy-start | bytes 196
  246.4 3.1 copy-start.1
  252.4 2.2 copy-start.2
  267.1 3.1 copy-start.1
  273.1 2.2 copy-start.2
  287.8 3.1 copy-start.1
  293.8 2.2 copy-start.2
  308.5 3.1 copy-start.1
  314.5 2.2 copy-start.2
  329.2 3.1 copy-start.1
  335.2 2.2 copy-start.2
  349.9 3.1 copy-start.1
  355.8 2.2 copy-start.2
  370.6 3.1 copy-start.1
  376.5 2.2 copy-start.2
  391.3 3.1 copy-start.1
  397.2 2.2 copy-start.2
  412.0 3.1 copy-start.1
  417.9 2.2 copy-start.2
  432.6 3.1 copy-start.1
  438.6 2.2 copy-start.2
  453.3 3.1 copy-start.1
  474.0 3.1 copy-start.1
  494.7 3.1 copy-start.1
  515.4 3.1 copy-start.1
  536.1 3.1 copy-start.1
  556.8 3.1 copy-start.1
  (6 other events, 13.1 us)
Sparse Core Ops, SparseCore 0:
  9.5 221.5 all-gather.1
where the time goes:
time: 642 us; the launch traced here: 639 us
  waiting for transfers between devices  225 us (35%)
  local copies, waits for them, and re-layouts  129 us (20%)
  loops' own time  127 us (20%)
  matrix products  90.1 us (14%)
  blocking collectives  40.1 us (6%)
  other arithmetic  14.6 us (2%)
  between operations  13.5 us (2%)
    all_gather x1, waiting for transfers between devices, local(): lax.all_gather(b_three, 'col', axis=0, tiled=True)  224 us
    another operation x1, loops' own time, fold_peers(): return lax.fori_loop(0, count, visit, gamma)  127 us
    while x64, local copies, waits for them, and re-layouts  52 us
    dot_general x16, matrix products, pair_step(): addition = jnp.dot(weighted, right_slab, preferred_element_type=jnp.float32)  46.4 us
    all_to_all x1, blocking collectives, local(): lax.all_to_all(blocks, ('row', 'col'), split_axis=0, concat_axis=0, tiled...  40.1 us
    dot_general x16, matrix products, pair_step(): lax.dot_general(left_slab, right_slab, (((1,), (1,)), ((), ())), preferre...  38.7 us
    dynamic_slice x16, local copies, waits for them, and re-layouts, pair_step(): current = lax.dynamic_index_in_dim(gamma, own_slot, 0, keepdims=False)  31.6 us
  transfers between devices with their start and end apart: 1, of which 1 were waited for; matrix products, arithmetic and copies ran while one was open for 0% of the time, Pallas kernels for 0%

commit v1 on v0

--- a/solution.py
+++ b/solution.py
@@ -43,7 +43,12 @@
 
         return lax.fori_loop(0, count, visit, gamma)
 
-    gamma = fold_peers(gamma, lax.all_gather(b_three, "col", axis=0, tiled=True))
+    gamma = fold_peers(
+        gamma,
+        jnp.concatenate(
+            lax.all_to_all(jnp.stack([b_three] * lax.axis_size("col")), "col", 0, 0), axis=0
+        ),
+    )
     gamma_mo = gamma.astype(jnp.bfloat16)
     virt_local = virt_count // row_count
     aux_local = aux_count // peer_count

time: 642 us -> 956 us (1.49)
  waiting for transfers between devices: 225 us -> 564 us
  local copies, waits for them, and re-layouts: 129 us -> 99.2 us
  matrix products: 90.1 us -> 115 us
  loops' own time: 127 us -> 113 us
  between operations: 13.5 us -> 0.06 us
    all_to_all x0 -> x1, waiting for transfers between devices: none -> 564 us  [local(): lax.all_to_all(jnp.stack([b_three] * lax.axis_size('col')), 'col', 0, 0)]
    all_gather x1 -> x0, waiting for transfers between devices: 224 us -> none  [local(): lax.all_gather(b_three, 'col', axis=0, tiled=True)]
    while x64 -> x0, local copies, waits for them, and re-layouts: 52 us -> none
    dot_general x16, matrix products: 46.4 us -> 71 us  [pair_step(): addition = jnp.dot(weighted, right_slab, preferred_element_type=jnp.float32)]
    another operation x1, loops' own time: 127 us -> 113 us  [fold_peers(): return lax.fori_loop(0, count, visit, gamma)]
    another operation x0 -> x1, local copies, waits for them, and re-layouts: none -> 13.6 us  [local(): jnp.stack([b_three] * lax.axis_size('col'))]
    dot_general x16, local copies, waits for them, and re-layouts: 3.68 us -> 16.9 us  [pair_step(): lax.dot_general(left_slab, right_slab, (((1,), (1,)), ((), ())), preferre...]
where the time goes in v1:
time: 956 us; the launch traced here: 952 us
  waiting for transfers between devices  564 us (59%)
  matrix products  115 us (12%)
  loops' own time  113 us (12%)
  local copies, waits for them, and re-layouts  99.2 us (10%)
  blocking collectives  38.8 us (4%)
  other arithmetic  13.7 us (1%)
    all_to_all x1, waiting for transfers between devices, local(): lax.all_to_all(jnp.stack([b_three] * lax.axis_size('col')), 'col', 0, 0)  564 us
    another operation x1, loops' own time, fold_peers(): return lax.fori_loop(0, count, visit, gamma)  113 us
    dot_general x16, matrix products, pair_step(): addition = jnp.dot(weighted, right_slab, preferred_element_type=jnp.float32)  71 us
    all_to_all x1, blocking collectives, local(): lax.all_to_all(blocks, ('row', 'col'), split_axis=0, concat_axis=0, tiled...  38.8 us
    dot_general x16, matrix products, pair_step(): lax.dot_general(left_slab, right_slab, (((1,), (1,)), ((), ())), preferre...  38.7 us
    dynamic_slice x16, local copies, waits for them, and re-layouts, pair_step(): current = lax.dynamic_index_in_dim(gamma, own_slot, 0, keepdims=False)  29.2 us
  transfers between devices with their start and end apart: 1, of which 1 were waited for; matrix products, arithmetic and copies ran while one was open for 0% of the time, Pallas kernels for 0%

profile of v1, /device:TPU:1, one launch (start us, length us, event | category | flops | bytes accessed | tf_op | source)
XLA Modules:
  0.0 952.1 jit_solution(17124140610367806766)
XLA Ops:
  0.0 13.6 %stack.2 = bf16[16,2,384,1536]{3,2,1,0:T(8,128)(2,1)} broadcast(bf16[2,384,1536]{2,1,0:T(8,128)(2,1)} %param.8), dimensions={1,2,3} | broadcast | bytes 40108032 | tf_op jit(solution)/shard_map/stack | solution.py:49
  13.6 8.5 all-to-all-start
  22.1 564.2 %all-to-all-done = bf16[16,2,384,1536]{3,2,1,0:T(8,128)(2,1)} async-done(((bf16[16,2,384,1536]{3,2,1,0:T(8,128)(2,1)}), bf16[16,2,384,1536]{3,2,1,0:T(8,128)(2,1)}, u32[]{:S(2)}, u32[]{:S(2)}) %all-to-all-start) | async-done | bytes 37748768 | tf_op jit(solution)/shard_map/all_to_all | solution.py:49
  586.2 2.8 broadcast_in_dim.20
  589.0 297.4 %while.15 = (s32[]{:T(128)}, f32[2,384,1536]{2,1,0:T(8,128)}, s32[1,16,2]{1,2,0:T(2,128)S(1)}, s32[1,16]{1,0:T(1,128)S(1)}, bf16[2,384,1536]{2,1,0:T(8,128)(2,1)...) while((s32[]{:T(128)}, f32[2,384,1536]{2,1,0:T(8,128)}, ...), condition=%wide.region_1.2_spmd, body=%wide.region_0.1_spmd.sunk | while | flops 908181888 | bytes 15937601 | solution.py:44
  603.2 4.4 fusion.40
  621.8 4.4 fusion.40
  640.4 4.4 fusion.40
  658.9 4.4 fusion.40
  677.5 4.4 fusion.40
  696.1 4.4 fusion.40
  706.5 2.4 fusion.38
  714.7 4.4 fusion.40
  733.3 4.4 fusion.40
  751.9 4.4 fusion.40
  762.3 2.4 fusion.38
  770.5 4.4 fusion.40
  789.0 4.4 fusion.40
  807.6 4.4 fusion.40
  818.0 2.4 fusion.38
  826.2 4.4 fusion.40
  844.8 4.4 fusion.40
  863.4 4.4 fusion.40
  882.0 4.4 fusion.40
  886.4 4.0 convert_element_type.29
  890.4 4.9 reshape.28
  895.3 2.5 copy.17
  897.8 5.1 reshape.29
  903.0 2.4 copy.15
  905.4 38.8 %all_to_all.10 = bf16[128,2,4608]{2,1,0:T(2,128)(2,1)} all-to-all(bf16[128,2,4608]{2,1,0:T(2,128)(2,1)S(1)} %copy.15), channel_id=1, replica_groups=mesh['row'=8,'col'=16] {'row','col'}, dimensions={0} | all-to-all | bytes 4718592 | tf_op jit(solution)/shard_map/all_to_all | solution.py:60
  944.2 2.9 reshape.30
  947.1 5.0 convolution_convert_fusion
  (119 shorter events, 106.1 us)
Async XLA Ops:
  0.0 947.1 %copy-start = (bf16[768,256]{1,0:T(8,128)(2,1)S(1)}, bf16[768,256]{1,0:T(8,128)(2,1)}, u32[]{:S(2)}) copy-start(bf16[768,256]{1,0:T(8,128)(2,1)} %param.11) | copy-start | bytes 1179652
  13.6 572.6 %all-to-all-start = ((bf16[16,2,384,1536]{3,2,1,0:T(8,128)(2,1)}), bf16[16,2,384,1536]{3,2,1,0:T(8,128)(2,1)}, u32[]{:S(2)}, u32[]{:S(2)}) async-start(bf16[16,2,384,1536]{3,2,1,0:T(8,128)(2,1)} %stack.2), calls=%async_computation | async-start | bytes 75497472 | tf_op jit(solution)/shard_map/all_to_all | solution.py:49
  586.2 2.8 copy-start.1
  586.2 2.8 copy-start.2
  586.2 2.8 copy-start.3
  586.2 2.8 copy-start.4
